TPU v7x, 32 devices: a whole 2x2x4 slice. The times are simulated.
32 devices in a mesh: rep: 8 (over z, core), shard: 4 (over y, x).
Axes of the slice: x: 2, y: 2, z: 4, core: 2. Of those that a mesh axis runs over, the one named last changes fastest.
Arguments:
- tokens: bfloat16 [4096, 1536], P(('rep', 'shard')), may hold values from -6 to 6
- cotangent: bfloat16 [4096, 1536], P(('rep', 'shard')), may hold values from -6 to 6
- lengths: int32 [8], P('rep'), may hold values from 128 to 512, as said below
- gain_one: bfloat16 [1536], P('shard'), may hold values from 0.5 to 1.5
- w_query: bfloat16 [1536, 1536], P('shard'), may hold values from -0.15625 to 0.15625
- w_key: bfloat16 [1536, 1536], P('shard'), may hold values from -0.15625 to 0.15625
- w_value: bfloat16 [1536, 1536], P('shard'), may hold values from -0.15625 to 0.15625
- w_path: bfloat16 [1536, 1536], P('shard'), may hold values from -0.15625 to 0.15625
- w_beta: bfloat16 [1536, 12], P('shard'), may hold values from -0.15625 to 0.15625
- w_out: bfloat16 [1536, 1536], P('shard'), may hold values from -0.625 to 0.625
- gain_two: bfloat16 [1536], P('shard'), may hold values from 0.5 to 1.5
- w_gate: bfloat16 [1536, 4096], P('shard'), may hold values from -0.15625 to 0.15625
- w_up: bfloat16 [1536, 4096], P('shard'), may hold values from -0.15625 to 0.15625
- w_down: bfloat16 [4096, 1536], P('shard'), may hold values from -0.09375 to 0.09375
Outputs:
- output: bfloat16 [4096, 1536], P(('rep', 'shard'))
- input_grad: bfloat16 [4096, 1536], P(('rep', 'shard'))
- grad_gain_one: float32 [1536], P('shard')
- grad_w_query: float32 [1536, 1536], P('shard')
- grad_w_key: float32 [1536, 1536], P('shard')
- grad_w_value: float32 [1536, 1536], P('shard')
- grad_w_path: float32 [1536, 1536], P('shard')
- grad_w_beta: float32 [1536, 12], P('shard')
- grad_w_out: float32 [1536, 1536], P('shard')
- grad_gain_two: float32 [1536], P('shard')
- grad_w_gate: float32 [1536, 4096], P('shard')
- grad_w_up: float32 [1536, 4096], P('shard')
- grad_w_down: float32 [4096, 1536], P('shard')
- rms_input: float32 [], replicated
- rms_attn: float32 [], replicated
- rms_feed: float32 [], replicated
Inputs may be any that keep to these rules, and one draw needn't show every extreme that they name: Sequence r fills the first lengths[r] of its 512 slots; at least one sequence fills all of them.
All inputs are finite; a program needn't handle non-finite values.
Results may differ from a plain program's by a relative error of at most 0.02.
Values may be sent and summed in bfloat16 or wider, within the bound.
No kernel may reach another device: no remote copies, remote signals or barrier semaphores. Data moves between devices by JAX's collectives and lax.ppermute only.
A program may use at most 320 MiB of HBM per device.

v0:
```python
import jax
import jax.numpy as jnp
from jax import lax
from jax.sharding import PartitionSpec as P

eps = 1e-06
highest = lax.Precision.HIGHEST


def rms_norm(value, gain_vec):
    factor = lax.rsqrt(jnp.mean(value * value, axis=-1, keepdims=True) + eps)
    return value * factor * gain_vec


def unit_rows(raw):
    return raw * lax.rsqrt(jnp.sum(raw * raw, axis=-1, keepdims=True) + eps)


def rounded(value):
    return lax.optimization_barrier(value.astype(jnp.bfloat16)).astype(jnp.float32)


def round_pass(value):
    return value + lax.stop_gradient(rounded(value) - value)


def split_heads(matrix, head_count):
    return matrix.reshape(matrix.shape[0], head_count, -1).transpose(1, 0, 2)


def join_heads(matrix):
    return matrix.transpose(1, 0, 2).reshape(matrix.shape[1], -1)


def mul_low(left, right):
    return jnp.dot(left, right, preferred_element_type=jnp.float32)


def back_mul(grad_rows, weight):
    return jnp.einsum("tg,fg->tf", grad_rows, weight, preferred_element_type=jnp.float32)


def weight_grad(left, right):
    return jnp.einsum("tf,tg->fg", left, right, preferred_element_type=jnp.float32)


def masks(block_len):
    row_ids = jnp.arange(block_len)[:, None]
    col_ids = jnp.arange(block_len)[None, :]
    return (col_ids < row_ids, col_ids <= row_ids)


def block_system(direction, beta_rate):
    block_len = direction.shape[1]
    strictly, up_to = masks(block_len)
    gram = jnp.einsum("htd,hsd->hts", direction, direction, precision=highest)
    return jnp.eye(block_len, dtype=jnp.float32)[None] + jnp.where(
        strictly[None], gram * beta_rate[:, None, :], 0.0
    )


def own_context(keyset, values, direction, beta_rate):
    system = block_system(direction, beta_rate)
    strictly, up_to = masks(keyset.shape[1])
    coupled = jnp.where(
        strictly[None], jnp.einsum("htd,hjd->htj", direction, keyset, precision=highest), 0.0
    )
    solved = jax.scipy.linalg.solve_triangular(system, coupled, lower=True, unit_diagonal=True)
    scaled_dir = direction * beta_rate[:, :, None]
    key_end = keyset - jnp.einsum("htj,htd->hjd", solved, scaled_dir, precision=highest)
    through = jax.scipy.linalg.solve_triangular(system, direction, lower=True, unit_diagonal=True)
    block_map = jnp.eye(direction.shape[2], dtype=jnp.float32)[None] - jnp.einsum(
        "htm,htn->hmn", scaled_dir, through, precision=highest
    )
    return (join_heads(key_end), join_heads(values), block_map[None])


def attend(
    queries, keyset, values, direction, beta_rate, key_far, value_far, maps_far, my_block, length
):
    head_count, block_len, head_width = queries.shape
    blocks = maps_far.shape[0]
    score_scale = head_width ** (-0.5)
    strictly, up_to = masks(block_len)
    system = block_system(direction, beta_rate)
    coupled = jnp.where(
        strictly[None], jnp.einsum("htd,hjd->htj", direction, keyset, precision=highest), 0.0
    )
    solved = jax.scipy.linalg.solve_triangular(system, coupled, lower=True, unit_diagonal=True)
    crossing = (
        jnp.where(
            up_to[None], jnp.einsum("hid,htd->hit", queries, direction, precision=highest), 0.0
        )
        * beta_rate[:, None, :]
    )
    near_scores = (
        jnp.einsum("hid,hjd->hij", queries, keyset, precision=highest)
        - jnp.einsum("hit,htj->hij", crossing, solved, precision=highest)
    ) * score_scale
    back_solved = jax.scipy.linalg.solve_triangular(
        system, crossing.transpose(0, 2, 1), lower=True, trans=1, unit_diagonal=True
    )
    moved = queries - jnp.einsum("hti,htd->hid", back_solved, direction, precision=highest)

    def advance(carried, item_pair):
        block_map, index = item_pair
        updated = jnp.einsum("hid,hde->hie", carried, block_map, precision=highest)
        return (jnp.where(index < my_block, updated, carried), carried)

    unused, reached = lax.scan(advance, moved, (maps_far, jnp.arange(blocks)), reverse=True)
    far_keys = key_far.reshape(blocks, block_len, head_count, head_width)
    far_values = value_far.reshape(blocks, block_len, head_count, head_width)
    far_scores = jnp.einsum("ehid,ejhd->ehij", reached, far_keys, precision=highest) * score_scale
    positions = jnp.arange(block_len)
    near_ok = up_to[None] & ((my_block * block_len + positions)[None, None, :] < length)
    block_ids = jnp.arange(blocks)
    far_ok = (block_ids[:, None, None, None] < my_block) & (
        (block_ids[:, None] * block_len + positions[None, :])[:, None, None, :] < length
    )
    near_masked = jnp.where(near_ok, near_scores, -1e30)
    far_masked = jnp.where(far_ok, far_scores, -1e30)
    row_max = jnp.maximum(jnp.max(near_masked, axis=2), jnp.max(far_masked, axis=(0, 3)))[
        :, :, None
    ]
    row_total = jnp.sum(jnp.where(near_ok, jnp.exp(near_masked - row_max), 0.0), axis=2) + jnp.sum(
        jnp.where(far_ok, jnp.exp(far_masked - row_max[None]), 0.0), axis=(0, 3)
    )
    log_total = row_max + jnp.log(row_total)[:, :, None]
    near_probs = round_pass(jnp.where(near_ok, jnp.exp(near_masked - log_total), 0.0))
    far_probs = round_pass(jnp.where(far_ok, jnp.exp(far_masked - log_total[None]), 0.0))
    return jnp.einsum("hij,hjd->hid", near_probs, values, precision=highest) + jnp.einsum(
        "ehij,ejhd->hid", far_probs, far_values, precision=highest
    )


def per_device(
    tokens,
    cotangent,
    lengths,
    gain_one,
    w_query,
    w_key,
    w_value,
    w_path,
    w_beta,
    w_out,
    gain_two,
    w_gate,
    w_up,
    w_down,
):
    gain_a, query_w, key_w, value_w, path_w, beta_w, out_w, gain_b, gate_w, up_w, down_w = (
        lax.all_gather(gain_one, "shard", axis=0, tiled=True),
        lax.all_gather(w_query, "shard", axis=0, tiled=True),
        lax.all_gather(w_key, "shard", axis=0, tiled=True),
        lax.all_gather(w_value, "shard", axis=0, tiled=True),
        lax.all_gather(w_path, "shard", axis=0, tiled=True),
        lax.all_gather(w_beta, "shard", axis=0, tiled=True),
        lax.all_gather(w_out, "shard", axis=0, tiled=True),
        lax.all_gather(gain_two, "shard", axis=0, tiled=True),
        lax.all_gather(w_gate, "shard", axis=0, tiled=True),
        lax.all_gather(w_up, "shard", axis=0, tiled=True),
        lax.all_gather(w_down, "shard", axis=0, tiled=True),
    )
    block_len = tokens.shape[0]
    width = tokens.shape[1]
    head_count = beta_w.shape[1]
    my_block = lax.axis_index("shard")
    length = lengths[0]
    live_mask = (my_block * block_len + jnp.arange(block_len) < length).astype(jnp.float32)[:, None]
    stream_in = tokens.astype(jnp.float32)
    normed_f, norm_pull = jax.vjp(rms_norm, stream_in, gain_a.astype(jnp.float32))
    normed = normed_f.astype(jnp.bfloat16)
    queries = split_heads(rounded(mul_low(normed, query_w)), head_count)
    keyset = split_heads(rounded(mul_low(normed, key_w)), head_count)
    values_h = split_heads(rounded(mul_low(normed, value_w)), head_count)
    raw = mul_low(normed, path_w).reshape(block_len, head_count, -1)
    direction_f, unit_pull = jax.vjp(unit_rows, raw)
    direction = rounded(direction_f).transpose(1, 0, 2)
    beta_rate = 2.0 * jax.nn.sigmoid(mul_low(normed, beta_w))
    (key_end, value_own, map_own), context_pull = jax.vjp(
        own_context, keyset, values_h, direction, beta_rate.T
    )
    key_far, value_far, maps_far = (
        lax.all_gather(key_end.astype(jnp.bfloat16), "shard", axis=0, tiled=True).astype(
            key_end.dtype
        ),
        lax.all_gather(value_own.astype(jnp.bfloat16), "shard", axis=0, tiled=True).astype(
            value_own.dtype
        ),
        lax.all_gather(map_own.astype(jnp.bfloat16), "shard", axis=0, tiled=True).astype(
            map_own.dtype
        ),
    )

    def local_attend(
        queries, keyset, values_h, direction, beta_heads, key_far, value_far, maps_far
    ):
        return attend(
            queries,
            keyset,
            values_h,
            direction,
            beta_heads,
            key_far,
            value_far,
            maps_far,
            my_block,
            length,
        )

    heads_out, attend_pull = jax.vjp(
        local_attend,
        queries,
        keyset,
        values_h,
        direction,
        beta_rate.T,
        key_far,
        value_far,
        maps_far,
    )
    mixed = join_heads(heads_out).astype(jnp.bfloat16)
    attn_out = mul_low(mixed, out_w)
    stream = stream_in + live_mask * attn_out
    normed_two_f, norm_two_pull = jax.vjp(rms_norm, stream, gain_b.astype(jnp.float32))
    normed_two = normed_two_f.astype(jnp.bfloat16)
    gate_pre = mul_low(normed_two, gate_w)
    up_pre = mul_low(normed_two, up_w)
    gate_sig = jax.nn.sigmoid(gate_pre)
    hidden = (gate_pre * gate_sig * up_pre).astype(jnp.bfloat16)
    feed_out = mul_low(hidden, down_w)
    output = (live_mask * (stream + feed_out)).astype(jnp.bfloat16)
    cot_rows = cotangent.astype(jnp.float32) * live_mask
    d_feed = cot_rows.astype(jnp.bfloat16)
    d_hidden = back_mul(d_feed, down_w)
    d_gate = (d_hidden * up_pre * gate_sig * (1.0 + gate_pre * (1.0 - gate_sig))).astype(
        jnp.bfloat16
    )
    d_up = (d_hidden * gate_pre * gate_sig).astype(jnp.bfloat16)
    d_normed_two = back_mul(d_gate, gate_w) + back_mul(d_up, up_w)
    d_stream_norm, grad_gain_b = norm_two_pull(d_normed_two)
    d_stream = cot_rows + d_stream_norm
    d_attn = (live_mask * d_stream).astype(jnp.bfloat16)
    d_mixed = split_heads(rounded(back_mul(d_attn, out_w)), head_count)
    (
        d_queries,
        d_keys_near,
        d_values_near,
        d_dir_near,
        d_beta_near,
        d_key_far,
        d_value_far,
        d_maps_far,
    ) = attend_pull(d_mixed)
    d_key_end, d_value_own, d_map_own = (
        lax.psum_scatter(
            d_key_far.astype(jnp.bfloat16), "shard", scatter_dimension=0, tiled=True
        ).astype(jnp.float32),
        lax.psum_scatter(
            d_value_far.astype(jnp.bfloat16), "shard", scatter_dimension=0, tiled=True
        ).astype(jnp.float32),
        lax.psum_scatter(
            d_maps_far.astype(jnp.bfloat16), "shard", scatter_dimension=0, tiled=True
        ).astype(jnp.float32),
    )
    d_keys_ctx, d_values_ctx, d_dir_ctx, d_beta_ctx = context_pull(
        (d_key_end, d_value_own, d_map_own)
    )
    d_query_b = join_heads(d_queries).astype(jnp.bfloat16)
    d_key_b = join_heads(d_keys_near + d_keys_ctx).astype(jnp.bfloat16)
    d_value_b = join_heads(d_values_near + d_values_ctx).astype(jnp.bfloat16)
    (d_raw,) = unit_pull((d_dir_near + d_dir_ctx).transpose(1, 0, 2))
    d_raw_b = d_raw.reshape(block_len, -1).astype(jnp.bfloat16)
    d_beta_total = (d_beta_near + d_beta_ctx).T
    d_logit_b = (d_beta_total * beta_rate * (1.0 - 0.5 * beta_rate)).astype(jnp.bfloat16)
    d_normed = (
        back_mul(d_query_b, query_w)
        + back_mul(d_key_b, key_w)
        + back_mul(d_value_b, value_w)
        + back_mul(d_raw_b, path_w)
        + back_mul(d_logit_b, beta_w)
    )
    d_stream_in, grad_gain_a = norm_pull(d_normed)
    input_grad = (d_stream_in + d_stream).astype(jnp.bfloat16)
    g_query = weight_grad(normed, d_query_b)
    g_key = weight_grad(normed, d_key_b)
    g_value = weight_grad(normed, d_value_b)
    g_path = weight_grad(normed, d_raw_b)
    g_beta = weight_grad(normed, d_logit_b)
    g_out = weight_grad(mixed, d_attn)
    g_gate = weight_grad(normed_two, d_gate)
    g_up = weight_grad(normed_two, d_up)
    g_down = weight_grad(hidden, d_feed)
    part_sums = (
        lax.psum_scatter(
            grad_gain_a.astype(jnp.bfloat16), "shard", scatter_dimension=0, tiled=True
        ).astype(jnp.float32),
        lax.psum_scatter(
            g_query.astype(jnp.bfloat16), "shard", scatter_dimension=0, tiled=True
        ).astype(jnp.float32),
        lax.psum_scatter(
            g_key.astype(jnp.bfloat16), "shard", scatter_dimension=0, tiled=True
        ).astype(jnp.float32),
        lax.psum_scatter(
            g_value.astype(jnp.bfloat16), "shard", scatter_dimension=0, tiled=True
        ).astype(jnp.float32),
        lax.psum_scatter(
            g_path.astype(jnp.bfloat16), "shard", scatter_dimension=0, tiled=True
        ).astype(jnp.float32),
        lax.psum_scatter(
            g_beta.astype(jnp.bfloat16), "shard", scatter_dimension=0, tiled=True
        ).astype(jnp.float32),
        lax.psum_scatter(
            g_out.astype(jnp.bfloat16), "shard", scatter_dimension=0, tiled=True
        ).astype(jnp.float32),
        lax.psum_scatter(
            grad_gain_b.astype(jnp.bfloat16), "shard", scatter_dimension=0, tiled=True
        ).astype(jnp.float32),
        lax.psum_scatter(
            g_gate.astype(jnp.bfloat16), "shard", scatter_dimension=0, tiled=True
        ).astype(jnp.float32),
        lax.psum_scatter(
            g_up.astype(jnp.bfloat16), "shard", scatter_dimension=0, tiled=True
        ).astype(jnp.float32),
        lax.psum_scatter(
            g_down.astype(jnp.bfloat16), "shard", scatter_dimension=0, tiled=True
        ).astype(jnp.float32),
    )
    owned = (
        lax.psum(part_sums[0].astype(jnp.bfloat16), "rep").astype(jnp.float32),
        lax.psum(part_sums[1].astype(jnp.bfloat16), "rep").astype(jnp.float32),
        lax.psum(part_sums[2].astype(jnp.bfloat16), "rep").astype(jnp.float32),
        lax.psum(part_sums[3].astype(jnp.bfloat16), "rep").astype(jnp.float32),
        lax.psum(part_sums[4].astype(jnp.bfloat16), "rep").astype(jnp.float32),
        lax.psum(part_sums[5].astype(jnp.bfloat16), "rep").astype(jnp.float32),
        lax.psum(part_sums[6].astype(jnp.bfloat16), "rep").astype(jnp.float32),
        lax.psum(part_sums[7].astype(jnp.bfloat16), "rep").astype(jnp.float32),
        lax.psum(part_sums[8].astype(jnp.bfloat16), "rep").astype(jnp.float32),
        lax.psum(part_sums[9].astype(jnp.bfloat16), "rep").astype(jnp.float32),
        lax.psum(part_sums[10].astype(jnp.bfloat16), "rep").astype(jnp.float32),
    )
    sq_input, sq_attn, sq_feed, live_total = lax.psum(
        (
            jnp.sum(live_mask * stream_in * stream_in),
            jnp.sum(live_mask * attn_out * attn_out),
            jnp.sum(live_mask * feed_out * feed_out),
            jnp.sum(live_mask),
        ),
        ("rep", "shard"),
    )
    denom = live_total * width
    return (
        output,
        input_grad,
        owned[0],
        owned[1],
        owned[2],
        owned[3],
        owned[4],
        owned[5],
        owned[6],
        owned[7],
        owned[8],
        owned[9],
        owned[10],
        jnp.sqrt(sq_input / denom),
        jnp.sqrt(sq_attn / denom),
        jnp.sqrt(sq_feed / denom),
    )


def solution(mesh):
    return jax.shard_map(
        per_device,
        mesh=mesh,
        in_specs=(
            P(("rep", "shard"), None),
            P(("rep", "shard"), None),
            P("rep"),
            P("shard"),
            P("shard", None),
            P("shard", None),
            P("shard", None),
            P("shard", None),
            P("shard", None),
            P("shard", None),
            P("shard"),
            P("shard", None),
            P("shard", None),
            P("shard", None),
        ),
        out_specs=(
            P(("rep", "shard"), None),
            P(("rep", "shard"), None),
            P("shard"),
            P("shard", None),
            P("shard", None),
            P("shard", None),
            P("shard", None),
            P("shard", None),
            P("shard", None),
            P("shard"),
            P("shard", None),
            P("shard", None),
            P("shard", None),
            P(),
            P(),
            P(),
        ),
        check_vma=False,
    )
```

profile of v0, /device:TPU:0, one launch (start us, length us, event | category | flops | bytes accessed | tf_op | source)
XLA Modules:
  0.0 1988.5 jit_solution(15971856994298718647)
XLA Ops:
  10.1 9.5 all-gather.1
  19.6 8.5 all_gather.46
  29.4 40.5 %all-gather.19.cloned.1.call-done = bf16[1536,1536]{1,0:T(8,128)(2,1)} async-done(((bf16[384,1536]{1,0:T(8,128)(2,1)}), bf16[1536,1536]{1,0:T(8,128)(2,1)}) %all-gather.19.cloned.1.call-update) | async-done | bytes 4718608 | tf_op jit(solution)/shard_map/all_gather | solution.py:157
  76.4 117.9 %custom-call.16 = f32[12,1,128,128]{2,3,1,0:T(8,128)S(1)} custom-call(f32[12,1,128,128]{3,2,1,0:T(8,128)S(1)} %add_bitcast_fusion), custom_call_target="InvertDiagBlocksLowerTriangular" | custom-call | tf_op jit(solution)/shard_map/jvp(jit(_solve_triangular))/vmap()/triangular_solve/custom-call.1 | solution.py:89
  216.0 8.1 all-gather.2
  228.1 20.2 %all-gather.15.cloned.1.call-done = bf16[1536,1536]{1,0:T(8,128)(2,1)} async-done(((bf16[384,1536]{1,0:T(8,128)(2,1)}), bf16[1536,1536]{1,0:T(8,128)(2,1)}) %all-gather.15.cloned.1.call-update) | async-done | bytes 4718608 | tf_op jit(solution)/shard_map/all_gather | solution.py:154
  263.0 18.5 all-gather.35.cloned.1.call-done
  285.0 29.7 %all-gather.21.cloned.1.call-done = bf16[512,1536]{0,1:T(8,128)(2,1)} async-done(((bf16[128,1536]{0,1:T(8,128)(2,1)}), bf16[512,1536]{0,1:T(8,128)(2,1)}) %all-gather.21.cloned.1.call-update) | async-done | bytes 1572880 | tf_op jit(solution)/shard_map/all_gather | solution.py:185
  321.8 19.7 while.31
  371.0 36.0 %all-gather.27.cloned.1.call-done = bf16[1536,1536]{1,0:T(8,128)(2,1)} async-done(((bf16[384,1536]{1,0:T(8,128)(2,1)}), bf16[1536,1536]{1,0:T(8,128)(2,1)}) %all-gather.27.cloned.1.call-update) | async-done | bytes 4718608 | tf_op jit(solution)/shard_map/all_gather | solution.py:159
  413.2 118.2 %all-gather.29.cloned.1.call-done = bf16[1536,4096]{1,0:T(8,128)(2,1)} async-done(((bf16[384,4096]{1,0:T(8,128)(2,1)}), bf16[1536,4096]{1,0:T(8,128)(2,1)}) %all-gather.29.cloned.1.call-update) | async-done | bytes 12582928 | tf_op jit(solution)/shard_map/all_gather | solution.py:161
  531.4 7.8 fusion.203
  539.3 116.4 %all-gather.31.cloned.1.call-done = bf16[1536,4096]{1,0:T(8,128)(2,1)} async-done(((bf16[384,4096]{1,0:T(8,128)(2,1)}), bf16[1536,4096]{1,0:T(8,128)(2,1)}) %all-gather.31.cloned.1.call-update) | async-done | bytes 12582928 | tf_op jit(solution)/shard_map/all_gather | solution.py:162
  663.5 116.5 %all-gather.33.cloned.1.call-done = bf16[4096,1536]{1,0:T(8,128)(2,1)} async-done(((bf16[1024,1536]{1,0:T(8,128)(2,1)}), bf16[4096,1536]{1,0:T(8,128)(2,1)}) %all-gather.33.cloned.1.call-update) | async-done | bytes 12582928 | tf_op jit(solution)/shard_map/all_gather | solution.py:163
  780.1 10.2 multiply_convert_fusion
  790.4 10.2 fusion.205
  800.7 9.7 multiply_reduce_fusion
  810.4 8.0 fusion.81
  832.8 8.0 fusion.31
  856.2 8.4 fusion.188
  864.6 41.8 %while.32 = (s32[]{:T(128)}, f32[12,128,128]{2,1,0:T(8,128)}, bf16[4,12,128,128]{3,2,1,0:T(8,128)(2,1)}, f32[4,12,128,128]{3,2,1,0:T(8,128)}, pred[4]{0:T(512)(1...) while((s32[]{:T(128)}, f32[12,128,128]{2,1,0:T(8,128)}, ...), condition=%wide.region_16.19_spmd.clone, body=%wide.region_15.18_spmd.clone.sunk | while | flops 605552640 | bytes 7869556 | solution.py:110
  1022.4 41.7 %reduce-scatter.29.cloned.1.call-done = bf16[384,1536]{1,0:T(8,128)(2,1)} async-done(((bf16[1536,1536]{1,0:T(8,128)(2,1)}), bf16[384,1536]{1,0:T(8,128)(2,1)}) %reduce-scatter.29.cloned.1.call-update) | async-done | bytes 1179664 | tf_op jit(solution)/shard_map/reduce_scatter | solution.py:314
  1064.0 60.5 %reduce-scatter.23.cloned.1.call-done = bf16[384,1536]{1,0:T(8,128)(2,1)} async-done(((bf16[1536,1536]{1,0:T(8,128)(2,1)}), bf16[384,1536]{1,0:T(8,128)(2,1)}) %reduce-scatter.23.cloned.1.call-update) | async-done | bytes 1179664 | tf_op jit(solution)/shard_map/reduce_scatter | solution.py:302
  1124.6 60.6 %reduce-scatter.25.cloned.1.call-done = bf16[384,1536]{1,0:T(8,128)(2,1)} async-done(((bf16[1536,1536]{1,0:T(8,128)(2,1)}), bf16[384,1536]{1,0:T(8,128)(2,1)}) %reduce-scatter.25.cloned.1.call-update) | async-done | bytes 1179664 | tf_op jit(solution)/shard_map/reduce_scatter | solution.py:305
  1185.1 60.1 %reduce-scatter.27.cloned.1.call-done = bf16[384,1536]{1,0:T(8,128)(2,1)} async-done(((bf16[1536,1536]{1,0:T(8,128)(2,1)}), bf16[384,1536]{1,0:T(8,128)(2,1)}) %reduce-scatter.27.cloned.1.call-update) | async-done | bytes 1179664 | tf_op jit(solution)/shard_map/reduce_scatter | solution.py:308
  1245.2 123.7 %reduce-scatter.31.cloned.1.call-done = bf16[384,4096]{1,0:T(8,128)(2,1)} async-done(((bf16[1536,4096]{1,0:T(8,128)(2,1)}), bf16[384,4096]{1,0:T(8,128)(2,1)}) %reduce-scatter.31.cloned.1.call-update) | async-done | bytes 3145744 | tf_op jit(solution)/shard_map/reduce_scatter | solution.py:320
  1368.9 123.9 %reduce-scatter.33.cloned.1.call-done = bf16[384,4096]{1,0:T(8,128)(2,1)} async-done(((bf16[1536,4096]{1,0:T(8,128)(2,1)}), bf16[384,4096]{1,0:T(8,128)(2,1)}) %reduce-scatter.33.cloned.1.call-update) | async-done | bytes 3145744 | tf_op jit(solution)/shard_map/reduce_scatter | solution.py:323
  1492.8 123.9 %reduce-scatter.35.cloned.1.call-done = bf16[1024,1536]{1,0:T(8,128)(2,1)} async-done(((bf16[4096,1536]{1,0:T(8,128)(2,1)}), bf16[1024,1536]{1,0:T(8,128)(2,1)}) %reduce-scatter.35.cloned.1.call-update) | async-done | bytes 3145744 | tf_op jit(solution)/shard_map/reduce_scatter | solution.py:326
  1633.7 40.3 %all-reduce.3 = (f32[]{:T(128)}, f32[]{:T(128)}, f32[]{:T(128)}, f32[]{:T(128)}) all-reduce(f32[]{:T(128)} %get-tuple-element.278, f32[]{:T(128)} %get-tuple-element.326, f32[]{:T(128)} %get-tuple-element.280, f32[]{:T(128)} %get-tuple-element.279), channel_id=1, replica_groups=mesh['rep'=8,'shard'=4] {'rep','shard'}, use_global_device_ids=true, to_apply=%region_52.55 | all-reduce | flops 4 | bytes 32 | tf_op jit(solution)/shard_map/psum | solution.py:343
  1674.0 10.8 all-reduce.6
  1689.7 28.2 %all-reduce.4 = (bf16[384]{0:T(512)(128)(2,1)S(1)}, bf16[384,12]{0,1:T(8,128)(2,1)S(1)}, bf16[384]{0:T(512)(128)(2,1)S(1)}) all-reduce(bf16[384]{0:T(512)(128)(2,1)S(1)} %dynamic-slice.3, bf16[384,12]{0,1:T(8,128)(2,1)S(1)} %copy.335, bf16[384]{0:T(512)(128)(2,1)S(1)} %dynamic-slice.5), channel_id=1, replica_groups=mesh['rep'=8,'shard'=4] {'rep'}, use_global_device_ids=true, to_apply=%region_29.32 | all-reduce | flops 5376 | bytes 21504 | tf_op jit(solution)/shard_map/psum | solution.py:331
  1719.6 238.0 %all-reduce.9.cloned.1.call-done = (bf16[384,1536]{1,0:T(8,128)(2,1)}, bf16[384,1536]{1,0:T(8,128)(2,1)}, bf16[384,1536]{1,0:T(8,128)(2,1)}, bf16[384,1536]{1,0:...) async-done(((bf16[384,1536]{1,0:T(8,128)(2,1)}, bf16[384,1536]{1,0:T(8,128)(2,1)}, ...) | async-done | bytes 15335440 | tf_op jit(solution)/shard_map/psum | solution.py:332
  (545 shorter events, 347.8 us)
Async XLA Ops:
  7.2 62.7 %all-gather.19.cloned.1.call-start = ((), (), s32[]{:S(2)}) async-start(), calls=%async_computation.14 | async-start | bytes 5898240 | tf_op jit(solution)/shard_map/all_gather | solution.py:157
  7.9 191.4 %all-gather.17.cloned.1.call-start = ((), (), s32[]{:S(2)}) async-start(), calls=%async_computation.13 | async-start | bytes 5898240 | tf_op jit(solution)/shard_map/all_gather | solution.py:155
  8.7 198.7 %all-gather.23.cloned.1.call-start = ((), (), s32[]{:S(2)}) async-start(), calls=%async_computation.16 | async-start | bytes 5898240 | tf_op jit(solution)/shard_map/all_gather | solution.py:156
  9.4 238.9 %all-gather.15.cloned.1.call-start = ((), (), s32[]{:S(2)}) async-start(), calls=%async_computation.12 | async-start | bytes 5898240 | tf_op jit(solution)/shard_map/all_gather | solution.py:154
  10.0 271.5 %all-gather.35.cloned.1.call-start = ((), (), s32[]{:S(2)}) async-start(), calls=%async_computation.30 | async-start | bytes 1966080 | tf_op jit(solution)/shard_map/all_gather | solution.py:191
  28.2 46.1 %copy-start.116 = (bf16[1536,12]{0,1:T(8,128)(2,1)}, bf16[1536,12]{0,1:T(8,128)(2,1)S(1)}, u32[]{:S(2)}) copy-start(bf16[1536,12]{0,1:T(8,128)(2,1)S(1)} %all_gather.46) | copy-start | bytes 110596
  29.0 170.4 %copy-start.108 = (f32[128]{0:T(128)}, f32[128]{0:T(128)S(1)}, u32[]{:S(2)}) copy-start(f32[128]{0:T(128)S(1)} %fusion.179) | copy-start | bytes 1540
  74.6 124.3 %copy-start.114 = (f32[128,12]{0,1:T(8,128)}, f32[128,12]{0,1:T(8,128)S(1)}, u32[]{:S(2)}) copy-start(f32[128,12]{0,1:T(8,128)S(1)} %multiply_reduce_fusion.7) | copy-start | bytes 18436
  194.3 60.0 %copy-start = (f32[12,1,128,128]{2,3,1,0:T(8,128)}, f32[12,1,128,128]{2,3,1,0:T(8,128)S(1)}, u32[]{:S(2)}) copy-start(f32[12,1,128,128]{2,3,1,0:T(8,128)S(1)} %custom-call.16) | copy-start | bytes 2359300
  199.0 115.6 %all-gather.21.cloned.1.call-start = ((), (), s32[]{:S(2)}) async-start(), calls=%async_computation.15 | async-start | bytes 1966080 | tf_op jit(solution)/shard_map/all_gather | solution.py:185
  203.2 57.3 %copy-start.16 = (bf16[128,1536]{0,1:T(8,128)(2,1)}, bf16[128,1536]{0,1:T(8,128)(2,1)S(1)}, u32[]{:S(2)}) copy-start(bf16[128,1536]{0,1:T(8,128)(2,1)S(1)} %copy.185) | copy-start | bytes 1179652
  204.9 53.4 %copy-start.9 = (f32[12,128,128]{2,1,0:T(8,128)}, f32[12,128,128]{2,1,0:T(8,128)S(1)}, u32[]{:S(2)}) copy-start(f32[12,128,128]{2,1,0:T(8,128)S(1)} %fusion.105) | copy-start | bytes 2359300
  207.4 143.5 %all-gather.25.cloned.1.call-start = ((), (), s32[]{:S(2)}) async-start(), calls=%async_computation.17 | async-start | bytes 1966080 | tf_op jit(solution)/shard_map/all_gather | solution.py:188
  211.4 195.7 %all-gather.27.cloned.1.call-start = ((), (), s32[]{:S(2)}) async-start(), calls=%async_computation.18 | async-start | bytes 5898240 | tf_op jit(solution)/shard_map/all_gather | solution.py:159
  212.1 319.3 %all-gather.29.cloned.1.call-start = ((), (), s32[]{:S(2)}) async-start(), calls=%async_computation.19 | async-start | bytes 15728640 | tf_op jit(solution)/shard_map/all_gather | solution.py:161
  212.9 442.8 %all-gather.31.cloned.1.call-start = ((), (), s32[]{:S(2)}) async-start(), calls=%async_computation.20 | async-start | bytes 15728640 | tf_op jit(solution)/shard_map/all_gather | solution.py:162
  213.5 566.6 %all-gather.33.cloned.1.call-start = ((), (), s32[]{:S(2)}) async-start(), calls=%async_computation.21 | async-start | bytes 15728640 | tf_op jit(solution)/shard_map/all_gather | solution.py:163
  214.2 724.2 %reduce-scatter.37.cloned.1.call-start = ((), (), s32[]{:S(2)}) async-start(), calls=%async_computation.31 | async-start | bytes 1966080
  843.5 108.3 %reduce-scatter.39.cloned.1.call-start = ((), (), s32[]{:S(2)}) async-start(), calls=%async_computation.32 | async-start | bytes 1966080
  856.0 116.3 %reduce-scatter.43.cloned.1.call-start = ((), (), s32[]{:S(2)}) async-start(), calls=%async_computation.34 | async-start | bytes 1966080
  906.5 115.9 %reduce-scatter.21.cloned.1.call-start = ((), (), s32[]{:S(2)}) async-start(), calls=%async_computation.22 | async-start | bytes 5898240 | tf_op jit(solution)/shard_map/reduce_scatter | solution.py:299
  923.5 140.5 %reduce-scatter.29.cloned.1.call-start = ((), (), s32[]{:S(2)}) async-start(), calls=%async_computation.26 | async-start | bytes 5898240 | tf_op jit(solution)/shard_map/reduce_scatter | solution.py:314
  928.4 196.2 %reduce-scatter.23.cloned.1.call-start = ((), (), s32[]{:S(2)}) async-start(), calls=%async_computation.23 | async-start | bytes 5898240 | tf_op jit(solution)/shard_map/reduce_scatter | solution.py:302
  951.7 233.4 %reduce-scatter.25.cloned.1.call-start = ((), (), s32[]{:S(2)}) async-start(), calls=%async_computation.24 | async-start | bytes 5898240 | tf_op jit(solution)/shard_map/reduce_scatter | solution.py:305
  960.9 284.3 %reduce-scatter.27.cloned.1.call-start = ((), (), s32[]{:S(2)}) async-start(), calls=%async_computation.25 | async-start | bytes 5898240 | tf_op jit(solution)/shard_map/reduce_scatter | solution.py:308
  996.8 372.2 %reduce-scatter.31.cloned.1.call-start = ((), (), s32[]{:S(2)}) async-start(), calls=%async_computation.27 | async-start | bytes 15728640 | tf_op jit(solution)/shard_map/reduce_scatter | solution.py:320
  1004.6 488.2 %reduce-scatter.33.cloned.1.call-start = ((), (), s32[]{:S(2)}) async-start(), calls=%async_computation.28 | async-start | bytes 15728640 | tf_op jit(solution)/shard_map/reduce_scatter | solution.py:323
  1012.2 604.5 %reduce-scatter.35.cloned.1.call-start = ((), (), s32[]{:S(2)}) async-start(), calls=%async_computation.29 | async-start | bytes 15728640 | tf_op jit(solution)/shard_map/reduce_scatter | solution.py:326
  1020.3 668.4 %reduce-scatter.41.cloned.1.call-start = ((), (), s32[]{:S(2)}) async-start(), calls=%async_computation.33 | async-start | bytes 491520
  1022.3 935.4 %all-reduce.9.cloned.1.call-start = ((), (), s32[]{:S(2)}) async-start(), calls=%async_computation.35 | async-start | bytes 30670848 | tf_op jit(solution)/shard_map/psum | solution.py:332
  1630.9 56.8 %copy-start.136 = (f32[128]{0:T(128)S(1)}, f32[128]{0:T(128)}, u32[]{:S(2)}) copy-start(f32[128]{0:T(128)} %copy-done.135) | copy-start | bytes 1540
  1630.9 56.8 %copy-start.23 = (f32[128,1536]{1,0:T(8,128)S(1)}, f32[128,1536]{1,0:T(8,128)}, u32[]{:S(2)}) copy-start(f32[128,1536]{1,0:T(8,128)} %copy-done.22) | copy-start | bytes 2359300
  (137 other events, 730.2 us)
Sparse Core Ops, SparseCore 0:
  9.9 60.0 all-gather.18
  71.8 58.0 all-gather.16
  131.7 57.6 all-gather.22
  191.1 57.1 all-gather.14
  250.5 30.9 all-gather.34
  283.8 30.8 all-gather.20
  317.1 30.9 all-gather.24
  349.9 57.0 all-gather.26
  408.9 122.5 all-gather.28
  533.1 122.5 all-gather.30
  657.5 122.5 all-gather.32
  843.6 30.9 reduce-scatter.36
  878.1 30.9 reduce-scatter.38
  912.5 30.9 reduce-scatter.42
  946.9 57.0 reduce-scatter.20
  1006.9 57.0 reduce-scatter.28
  1067.4 57.0 reduce-scatter.22
  1128.0 57.0 reduce-scatter.24
  1188.1 57.0 reduce-scatter.26
  1248.2 120.7 reduce-scatter.30
  1372.0 120.7 reduce-scatter.32
  1495.9 120.7 reduce-scatter.34
  1620.0 24.5 reduce-scatter.40
  1647.4 310.1 all-reduce.8
where the time goes:
time: 2000 us; the launch traced here: 1990 us
  waiting for transfers between devices  1330 us (66%)
  matrix products  278 us (14%)
  other arithmetic  163 us (8%)
  blocking collectives  105 us (5%)
  local copies, waits for them, and re-layouts  78.5 us (4%)
  between operations  24 us (1%)
    psum x1, waiting for transfers between devices, per_device(): lax.psum(part_sums[1].astype(jnp.bfloat16), 'rep').astype(jnp.float32)  238 us
    reduce_scatter x1, waiting for transfers between devices, per_device(): lax.psum_scatter(g_up.astype(jnp.bfloat16), 'shard', scatter_dimension=0,...  124 us
    reduce_scatter x1, waiting for transfers between devices, per_device(): lax.psum_scatter(g_down.astype(jnp.bfloat16), 'shard', scatter_dimension=...  124 us
    reduce_scatter x1, waiting for transfers between devices, per_device(): lax.psum_scatter(g_gate.astype(jnp.bfloat16), 'shard', scatter_dimension=...  124 us
    all_gather x1, waiting for transfers between devices, per_device(): lax.all_gather(w_gate, 'shard', axis=0, tiled=True)  118 us
    another operation x4, other arithmetic, attend(): jax.scipy.linalg.solve_triangular(system, coupled, lower=True, unit_diago...  118 us
    all_gather x1, waiting for transfers between devices, per_device(): lax.all_gather(w_down, 'shard', axis=0, tiled=True)  117 us
    all_gather x1, waiting for transfers between devices, per_device(): lax.all_gather(w_up, 'shard', axis=0, tiled=True)  116 us
  transfers between devices with their start and end apart: 24, of which 16 were waited for; matrix products, arithmetic and copies ran while one was open for 21% of the time, Pallas kernels for 0%

commit v1 on v0

--- a/solution.py
+++ b/solution.py
@@ -5,6 +5,22 @@
 
 eps = 1e-06
 highest = lax.Precision.HIGHEST
+
+
+def collect(x, axis, dim):
+    ways, here, step = (lax.axis_size(axis), lax.axis_index(axis), x.shape[dim])
+    shape = [n * ways if d == dim else n for d, n in enumerate(x.shape)]
+    full = lax.dynamic_update_slice_in_dim(jnp.zeros(shape, x.dtype), x, here * step, axis=dim)
+    going_up = going_down = x
+    for far in range(1, ways // 2 + 1):
+        going_up = lax.ppermute(going_up, axis, [(d, (d + 1) % ways) for d in range(ways)])
+        full = lax.dynamic_update_slice_in_dim(full, going_up, (here - far) % ways * step, axis=dim)
+        if 2 * far < ways:
+            going_down = lax.ppermute(going_down, axis, [(d, (d - 1) % ways) for d in range(ways)])
+            full = lax.dynamic_update_slice_in_dim(
+                full, going_down, (here + far) % ways * step, axis=dim
+            )
+    return full
 
 
 def rms_norm(value, gain_vec):
@@ -158,7 +174,7 @@
         lax.all_gather(w_beta, "shard", axis=0, tiled=True),
         lax.all_gather(w_out, "shard", axis=0, tiled=True),
         lax.all_gather(gain_two, "shard", axis=0, tiled=True),
-        lax.all_gather(w_gate, "shard", axis=0, tiled=True),
+        collect(w_gate, "shard", 0),
         lax.all_gather(w_up, "shard", axis=0, tiled=True),
         lax.all_gather(w_down, "shard", axis=0, tiled=True),
     )

time: 2000 us -> 2020 us (1.010)
  blocking collectives: 105 us -> 266 us
  waiting for transfers between devices: 1330 us -> 1170 us
  local copies, waits for them, and re-layouts: 78.5 us -> 111 us
    all_gather x1, blocking collectives: 8.08 us -> 169 us  [per_device(): lax.all_gather(gain_two, 'shard', axis=0, tiled=True)]
    all_gather x1 -> x0, waiting for transfers between devices: 118 us -> none  [per_device(): lax.all_gather(w_gate, 'shard', axis=0, tiled=True)]
    ppermute x0 -> x3, waiting for transfers between devices: none -> 107 us  [the longest x2 107 us: collect(): lax.ppermute(going_up, axis, [(d, (d + 1) % ways) for d in range(ways)])]
    all_gather x1, waiting for transfers between devices: 116 us -> 40.9 us  [per_device(): lax.all_gather(w_up, 'shard', axis=0, tiled=True)]
    reduce_scatter x1, waiting for transfers between devices: 0.02 us -> 60.5 us  [per_device(): lax.psum_scatter(g_query.astype(jnp.bfloat16), 'shard', scatter_dimension...]
    all_gather x1, waiting for transfers between devices: 36 us -> 0.01 us  [per_device(): lax.all_gather(w_out, 'shard', axis=0, tiled=True)]
    reduce_scatter x1, waiting for transfers between devices: 41.7 us -> 6.04 us  [per_device(): lax.psum_scatter(g_out.astype(jnp.bfloat16), 'shard', scatter_dimension=0...]
    all_gather x1, waiting for transfers between devices: 29.7 us -> 0.02 us  [per_device(): lax.all_gather(key_end.astype(jnp.bfloat16), 'shard', axis=0, tiled=True)]
  transfers between devices with their start and end apart: 24 -> 26, of which waited for: 16 -> 13; matrix products, arithmetic and copies ran while one was open for 21% -> 22% of each run, Pallas kernels for 0% -> 0%
where the time goes in v1:
time: 2020 us; the launch traced here: 2010 us
  waiting for transfers between devices  1170 us (58%)
  matrix products  273 us (14%)
  blocking collectives  266 us (13%)
  other arithmetic  161 us (8%)
  local copies, waits for them, and re-layouts  111 us (5%)
  between operations  23.7 us (1%)
    psum x1, waiting for transfers between devices, per_device(): lax.psum(part_sums[1].astype(jnp.bfloat16), 'rep').astype(jnp.float32)  238 us
    all_gather x1, blocking collectives, per_device(): lax.all_gather(gain_two, 'shard', axis=0, tiled=True)  169 us
    reduce_scatter x1, waiting for transfers between devices, per_device(): lax.psum_scatter(g_gate.astype(jnp.bfloat16), 'shard', scatter_dimension=...  124 us
    reduce_scatter x1, waiting for transfers between devices, per_device(): lax.psum_scatter(g_down.astype(jnp.bfloat16), 'shard', scatter_dimension=...  124 us
    reduce_scatter x1, waiting for transfers between devices, per_device(): lax.psum_scatter(g_up.astype(jnp.bfloat16), 'shard', scatter_dimension=0,...  124 us
    another operation x4, other arithmetic, attend(): jax.scipy.linalg.solve_triangular(system, coupled, lower=True, unit_diago...  118 us
    all_gather x1, waiting for transfers between devices, per_device(): lax.all_gather(w_down, 'shard', axis=0, tiled=True)  116 us
    ppermute x2, waiting for transfers between devices, collect(): lax.ppermute(going_up, axis, [(d, (d + 1) % ways) for d in range(ways)])  107 us
  transfers between devices with their start and end apart: 26, of which 13 were waited for; matrix products, arithmetic and copies ran while one was open for 22% of the time, Pallas kernels for 0%

profile of v1, /device:TPU:0, one launch (start us, length us, event | category | flops | bytes accessed | tf_op | source)
XLA Modules:
  0.0 2010.4 jit_solution(3507874786225423820)
XLA Ops:
  10.1 9.5 all-gather.1
  19.6 8.5 all_gather.43
  29.3 40.6 %all-gather.18.cloned.1.call-done = bf16[1536,1536]{1,0:T(8,128)(2,1)} async-done(((bf16[384,1536]{1,0:T(8,128)(2,1)}), bf16[1536,1536]{1,0:T(8,128)(2,1)}) %all-gather.18.cloned.1.call-update) | async-done | bytes 4718608 | tf_op jit(solution)/shard_map/all_gather | solution.py:173
  76.4 117.9 %custom-call.16 = f32[12,1,128,128]{2,3,1,0:T(8,128)S(1)} custom-call(f32[12,1,128,128]{3,2,1,0:T(8,128)S(1)} %add_bitcast_fusion), custom_call_target="InvertDiagBlocksLowerTriangular" | custom-call | tf_op jit(solution)/shard_map/jvp(jit(_solve_triangular))/vmap()/triangular_solve/custom-call.1 | solution.py:105
  216.5 107.2 %collective-permute-done = bf16[384,4096]{1,0:T(8,128)(2,1)} collective-permute-done((bf16[384,4096]{1,0:T(8,128)(2,1)}, bf16[384,4096]{1,0:T(8,128)(2,1)}, u32[]{:S(2)}, u32[]{:S(2)}) %collective-permute-start) | collective-permute-done | bytes 3145760 | tf_op jit(solution)/shard_map/ppermute | solution.py:16
  326.1 168.6 %all-gather.2 = bf16[4,1,384]{2,1,0:T(2,128)(2,1)S(1)} all-gather(bf16[1,1,384]{2,1,0:T(2,128)(2,1)S(1)} %reshape.387), channel_id=1, replica_groups=mesh['rep'=8,'shard'=4] {'shard'}, dimensions={0}, use_global_device_ids=true | all-gather | bytes 3840 | tf_op jit(solution)/shard_map/all_gather | solution.py:176
  497.9 6.5 broadcast_in_dim.214
  547.2 30.1 %while.31 = (s32[]{:T(128)}, f32[12,128,128]{1,2,0:T(8,128)}, f32[4,12,128,128]{2,3,1,0:T(8,128)}, pred[4]{0:T(512)(128)(4,1)}, s32[4]{0:T(128)}, /*index=5*/s32...) while((s32[]{:T(128)}, f32[12,128,128]{1,2,0:T(8,128)}, f32[4,12,128,128]{2,3,1,0:T(8,128)}, ...), condition=%wide.region_4.7_spmd, body=%wide.region_3.6_spmd.sunk | while | flops 302186496 | bytes 6291597 | solution.py:126
  612.1 40.9 %all-gather.28.cloned.1.call-done = bf16[1536,4096]{1,0:T(8,128)(2,1)} async-done(((bf16[384,4096]{1,0:T(8,128)(2,1)}), bf16[1536,4096]{1,0:T(8,128)(2,1)}) %all-gather.28.cloned.1.call-update) | async-done | bytes 12582928 | tf_op jit(solution)/shard_map/all_gather | solution.py:178
  653.0 7.8 fusion.203
  660.8 116.4 %all-gather.30.cloned.1.call-done = bf16[4096,1536]{1,0:T(8,128)(2,1)} async-done(((bf16[1024,1536]{1,0:T(8,128)(2,1)}), bf16[4096,1536]{1,0:T(8,128)(2,1)}) %all-gather.30.cloned.1.call-update) | async-done | bytes 12582928 | tf_op jit(solution)/shard_map/all_gather | solution.py:179
  777.2 10.3 fusion.171
  787.5 10.6 multiply_convert_fusion.1
  798.2 6.6 fusion.204
  804.9 10.4 multiply_reduce_fusion
  815.4 8.0 fusion.81
  838.3 8.0 fusion.31
  849.2 8.2 fusion.188
  857.4 42.1 %while.32 = (s32[]{:T(128)}, f32[12,128,128]{2,1,0:T(8,128)}, bf16[4,12,128,128]{3,2,1,0:T(8,128)(2,1)}, f32[4,12,128,128]{3,2,1,0:T(8,128)}, pred[4]{0:T(512)(1...) while((s32[]{:T(128)}, f32[12,128,128]{2,1,0:T(8,128)}, ...), condition=%wide.region_16.19_spmd.clone, body=%wide.region_15.18_spmd.clone.sunk | while | flops 605552640 | bytes 7869037 | solution.py:126
  1002.3 6.5 convolution_convert_fusion.1
  1010.2 6.7 convolution_convert_fusion
  1025.0 60.5 %reduce-scatter.21.cloned.1.call-done = bf16[384,1536]{1,0:T(8,128)(2,1)} async-done(((bf16[1536,1536]{1,0:T(8,128)(2,1)}), bf16[384,1536]{1,0:T(8,128)(2,1)}) %reduce-scatter.21.cloned.1.call-update) | async-done | bytes 1179664 | tf_op jit(solution)/shard_map/reduce_scatter | solution.py:315
  1085.5 60.0 %reduce-scatter.27.cloned.1.call-done = bf16[384,1536]{1,0:T(8,128)(2,1)} async-done(((bf16[1536,1536]{1,0:T(8,128)(2,1)}), bf16[384,1536]{1,0:T(8,128)(2,1)}) %reduce-scatter.27.cloned.1.call-update) | async-done | bytes 1179664 | tf_op jit(solution)/shard_map/reduce_scatter | solution.py:324
  1145.5 60.5 %reduce-scatter.25.cloned.1.call-done = bf16[384,1536]{1,0:T(8,128)(2,1)} async-done(((bf16[1536,1536]{1,0:T(8,128)(2,1)}), bf16[384,1536]{1,0:T(8,128)(2,1)}) %reduce-scatter.25.cloned.1.call-update) | async-done | bytes 1179664 | tf_op jit(solution)/shard_map/reduce_scatter | solution.py:321
  1206.1 60.6 %reduce-scatter.23.cloned.1.call-done = bf16[384,1536]{1,0:T(8,128)(2,1)} async-done(((bf16[1536,1536]{1,0:T(8,128)(2,1)}), bf16[384,1536]{1,0:T(8,128)(2,1)}) %reduce-scatter.23.cloned.1.call-update) | async-done | bytes 1179664 | tf_op jit(solution)/shard_map/reduce_scatter | solution.py:318
  1266.6 123.9 %reduce-scatter.31.cloned.1.call-done = bf16[384,4096]{1,0:T(8,128)(2,1)} async-done(((bf16[1536,4096]{1,0:T(8,128)(2,1)}), bf16[384,4096]{1,0:T(8,128)(2,1)}) %reduce-scatter.31.cloned.1.call-update) | async-done | bytes 3145744 | tf_op jit(solution)/shard_map/reduce_scatter | solution.py:336
  1390.5 123.7 %reduce-scatter.33.cloned.1.call-done = bf16[384,4096]{1,0:T(8,128)(2,1)} async-done(((bf16[1536,4096]{1,0:T(8,128)(2,1)}), bf16[384,4096]{1,0:T(8,128)(2,1)}) %reduce-scatter.33.cloned.1.call-update) | async-done | bytes 3145744 | tf_op jit(solution)/shard_map/reduce_scatter | solution.py:339
  1514.2 123.9 %reduce-scatter.35.cloned.1.call-done = bf16[1024,1536]{1,0:T(8,128)(2,1)} async-done(((bf16[4096,1536]{1,0:T(8,128)(2,1)}), bf16[1024,1536]{1,0:T(8,128)(2,1)}) %reduce-scatter.35.cloned.1.call-update) | async-done | bytes 3145744 | tf_op jit(solution)/shard_map/reduce_scatter | solution.py:342
  1655.1 40.3 %all-reduce.3 = (f32[]{:T(128)}, f32[]{:T(128)}, f32[]{:T(128)}, f32[]{:T(128)}) all-reduce(f32[]{:T(128)} %get-tuple-element.278, f32[]{:T(128)} %get-tuple-element.326, f32[]{:T(128)} %get-tuple-element.280, f32[]{:T(128)} %get-tuple-element.279), channel_id=1, replica_groups=mesh['rep'=8,'shard'=4] {'rep','shard'}, use_global_device_ids=true, to_apply=%region_52.55 | all-reduce | flops 4 | bytes 32 | tf_op jit(solution)/shard_map/psum | solution.py:359
  1698.2 10.8 all-reduce.6
  1711.2 28.2 %all-reduce.4 = (bf16[384]{0:T(512)(128)(2,1)S(1)}, bf16[384,12]{0,1:T(8,128)(2,1)S(1)}, bf16[384]{0:T(512)(128)(2,1)S(1)}) all-reduce(bf16[384]{0:T(512)(128)(2,1)S(1)} %dynamic-slice.3, bf16[384,12]{0,1:T(8,128)(2,1)S(1)} %copy.335, bf16[384]{0:T(512)(128)(2,1)S(1)} %dynamic-slice.5), channel_id=1, replica_groups=mesh['rep'=8,'shard'=4] {'rep'}, use_global_device_ids=true, to_apply=%region_29.32 | all-reduce | flops 5376 | bytes 21504 | tf_op jit(solution)/shard_map/psum | solution.py:347
  1741.1 238.1 %all-reduce.9.cloned.1.call-done = (bf16[384,1536]{1,0:T(8,128)(2,1)}, bf16[384,1536]{1,0:T(8,128)(2,1)}, bf16[384,1536]{1,0:T(8,128)(2,1)}, bf16[384,1536]{1,0:...) async-done(((bf16[384,1536]{1,0:T(8,128)(2,1)}, bf16[384,1536]{1,0:T(8,128)(2,1)}, ...) | async-done | bytes 15335440 | tf_op jit(solution)/shard_map/psum | solution.py:348
  (572 shorter events, 354.2 us)
Async XLA Ops:
  7.2 62.7 %all-gather.18.cloned.1.call-start = ((), (), s32[]{:S(2)}) async-start(), calls=%async_computation.14 | async-start | bytes 5898240 | tf_op jit(solution)/shard_map/all_gather | solution.py:173
  7.9 191.5 %all-gather.16.cloned.1.call-start = ((), (), s32[]{:S(2)}) async-start(), calls=%async_computation.13 | async-start | bytes 5898240 | tf_op jit(solution)/shard_map/all_gather | solution.py:171
  8.7 198.7 %all-gather.22.cloned.1.call-start = ((), (), s32[]{:S(2)}) async-start(), calls=%async_computation.16 | async-start | bytes 5898240 | tf_op jit(solution)/shard_map/all_gather | solution.py:172
  9.4 509.6 %all-gather.14.cloned.1.call-start = ((), (), s32[]{:S(2)}) async-start(), calls=%async_computation.12 | async-start | bytes 5898240 | tf_op jit(solution)/shard_map/all_gather | solution.py:170
  10.0 524.1 %all-gather.32.cloned.1.call-start = ((), (), s32[]{:S(2)}) async-start(), calls=%async_computation.29 | async-start | bytes 1966080 | tf_op jit(solution)/shard_map/all_gather | solution.py:207
  28.9 170.5 %copy-start.113 = (f32[128]{0:T(128)}, f32[128]{0:T(128)S(1)}, u32[]{:S(2)}) copy-start(f32[128]{0:T(128)S(1)} %fusion.179) | copy-start | bytes 1540
  74.6 124.4 %copy-start.118 = (f32[128,12]{0,1:T(8,128)}, f32[128,12]{0,1:T(8,128)S(1)}, u32[]{:S(2)}) copy-start(f32[128,12]{0,1:T(8,128)S(1)} %multiply_reduce_fusion.7) | copy-start | bytes 18436
  194.3 330.7 %copy-start = (f32[12,1,128,128]{2,3,1,0:T(8,128)}, f32[12,1,128,128]{2,3,1,0:T(8,128)S(1)}, u32[]{:S(2)}) copy-start(f32[12,1,128,128]{2,3,1,0:T(8,128)S(1)} %custom-call.16) | copy-start | bytes 2359300
  199.0 336.8 %all-gather.20.cloned.1.call-start = ((), (), s32[]{:S(2)}) async-start(), calls=%async_computation.15 | async-start | bytes 1966080 | tf_op jit(solution)/shard_map/all_gather | solution.py:201
  203.2 328.4 %copy-start.22 = (bf16[128,1536]{0,1:T(8,128)(2,1)}, bf16[128,1536]{0,1:T(8,128)(2,1)S(1)}, u32[]{:S(2)}) copy-start(bf16[128,1536]{0,1:T(8,128)(2,1)S(1)} %copy.185) | copy-start | bytes 1179652
  204.9 325.0 %copy-start.10 = (f32[12,128,128]{2,1,0:T(8,128)}, f32[12,128,128]{2,1,0:T(8,128)S(1)}, u32[]{:S(2)}) copy-start(f32[12,128,128]{2,1,0:T(8,128)S(1)} %fusion.105) | copy-start | bytes 2359300
  207.4 380.8 %all-gather.24.cloned.1.call-start = ((), (), s32[]{:S(2)}) async-start(), calls=%async_computation.17 | async-start | bytes 1966080 | tf_op jit(solution)/shard_map/all_gather | solution.py:204
  211.4 394.5 %all-gather.26.cloned.1.call-start = ((), (), s32[]{:S(2)}) async-start(), calls=%async_computation.18 | async-start | bytes 5898240 | tf_op jit(solution)/shard_map/all_gather | solution.py:175
  212.1 114.0 %copy-start.141 = (bf16[384]{0:T(512)(128)(2,1)S(1)}, bf16[384]{0:T(512)(128)(2,1)}, u32[]{:S(2)}) copy-start(bf16[384]{0:T(512)(128)(2,1)} %param.32) | copy-start | bytes 2308
  212.1 440.8 %all-gather.28.cloned.1.call-start = ((), (), s32[]{:S(2)}) async-start(), calls=%async_computation.19 | async-start | bytes 15728640 | tf_op jit(solution)/shard_map/all_gather | solution.py:178
  212.9 564.3 %all-gather.30.cloned.1.call-start = ((), (), s32[]{:S(2)}) async-start(), calls=%async_computation.20 | async-start | bytes 15728640 | tf_op jit(solution)/shard_map/all_gather | solution.py:179
  213.5 731.2 %reduce-scatter.37.cloned.1.call-start = ((), (), s32[]{:S(2)}) async-start(), calls=%async_computation.30 | async-start | bytes 1966080
  213.5 110.2 %collective-permute-start = (bf16[384,4096]{1,0:T(8,128)(2,1)}, bf16[384,4096]{1,0:T(8,128)(2,1)}, u32[]{:S(2)}, u32[]{:S(2)}) collective-permute-start(bf16[384,4096]{1,0:T(8,128)(2,1)} %param.33), channel_id=1, source_target_pairs={{0,1},{1,2},{2,3},{3,0},{4,5},{5,6},{6,7},{7,4},{8,9},{9,10},{10,1... | collective-permute-start | bytes 9437192 | tf_op jit(solution)/shard_map/ppermute | solution.py:16
  215.1 295.1 %collective-permute-start.1 = (bf16[384,4096]{1,0:T(8,128)(2,1)}, bf16[384,4096]{1,0:T(8,128)(2,1)}, u32[]{:S(2)}, u32[]{:S(2)}) collective-permute-start(bf16[384,4096]{1,0:T(8,128)(2,1)} %param.33), channel_id=1, source_target_pairs={{0,3},{1,0},{2,1},{3,2},{4,7},{5,4},{6,5},{7,6},{8,11},{9,8},{10,9... | collective-permute-start | bytes 9437192 | tf_op jit(solution)/shard_map/ppermute | solution.py:19
  323.7 190.4 %collective-permute-start.2 = (bf16[384,4096]{1,0:T(8,128)(2,1)}, bf16[384,4096]{1,0:T(8,128)(2,1)}, u32[]{:S(2)}, u32[]{:S(2)}) collective-permute-start(bf16[384,4096]{1,0:T(8,128)(2,1)} %collective-permute-done), channel_id=1, source_target_pairs={{0,1},{1,2},{2,3},{3,0},{4,5},{5,6},{6,7},{7,4},{8,9},{9,10},{10,1... | collective-permute-start | bytes 9437192 | tf_op jit(solution)/shard_map/ppermute | solution.py:16
  849.0 101.3 %reduce-scatter.43.cloned.1.call-start = ((), (), s32[]{:S(2)}) async-start(), calls=%async_computation.33 | async-start | bytes 1966080
  899.5 79.5 %reduce-scatter.39.cloned.1.call-start = ((), (), s32[]{:S(2)}) async-start(), calls=%async_computation.31 | async-start | bytes 1966080
  908.4 116.6 %reduce-scatter.29.cloned.1.call-start = ((), (), s32[]{:S(2)}) async-start(), calls=%async_computation.25 | async-start | bytes 5898240 | tf_op jit(solution)/shard_map/reduce_scatter | solution.py:330
  913.1 172.4 %reduce-scatter.21.cloned.1.call-start = ((), (), s32[]{:S(2)}) async-start(), calls=%async_computation.21 | async-start | bytes 5898240 | tf_op jit(solution)/shard_map/reduce_scatter | solution.py:315
  929.6 215.9 %reduce-scatter.27.cloned.1.call-start = ((), (), s32[]{:S(2)}) async-start(), calls=%async_computation.24 | async-start | bytes 5898240 | tf_op jit(solution)/shard_map/reduce_scatter | solution.py:324
  978.9 227.2 %reduce-scatter.25.cloned.1.call-start = ((), (), s32[]{:S(2)}) async-start(), calls=%async_computation.23 | async-start | bytes 5898240 | tf_op jit(solution)/shard_map/reduce_scatter | solution.py:321
  985.6 281.0 %reduce-scatter.23.cloned.1.call-start = ((), (), s32[]{:S(2)}) async-start(), calls=%async_computation.22 | async-start | bytes 5898240 | tf_op jit(solution)/shard_map/reduce_scatter | solution.py:318
  993.2 397.3 %reduce-scatter.31.cloned.1.call-start = ((), (), s32[]{:S(2)}) async-start(), calls=%async_computation.26 | async-start | bytes 15728640 | tf_op jit(solution)/shard_map/reduce_scatter | solution.py:336
  1001.1 513.1 %reduce-scatter.33.cloned.1.call-start = ((), (), s32[]{:S(2)}) async-start(), calls=%async_computation.27 | async-start | bytes 15728640 | tf_op jit(solution)/shard_map/reduce_scatter | solution.py:339
  1008.8 629.3 %reduce-scatter.35.cloned.1.call-start = ((), (), s32[]{:S(2)}) async-start(), calls=%async_computation.28 | async-start | bytes 15728640 | tf_op jit(solution)/shard_map/reduce_scatter | solution.py:342
  1017.0 693.3 %reduce-scatter.41.cloned.1.call-start = ((), (), s32[]{:S(2)}) async-start(), calls=%async_computation.32 | async-start | bytes 491520
  1018.9 960.3 %all-reduce.9.cloned.1.call-start = ((), (), s32[]{:S(2)}) async-start(), calls=%async_computation.34 | async-start | bytes 30670848 | tf_op jit(solution)/shard_map/psum | solution.py:348
  (148 other events, 961.6 us)
Sparse Core Ops, SparseCore 0:
  9.9 60.0 all-gather.17
  71.8 58.0 all-gather.15
  131.7 57.6 all-gather.21
  191.1 83.4 all-gather.13
  276.8 43.6 all-gather.31
  322.8 93.5 all-gather.19
  418.8 43.7 all-gather.23
  464.4 64.1 all-gather.25
  530.4 122.5 all-gather.27
  654.7 122.5 all-gather.29
  849.1 30.8 reduce-scatter.36
  899.6 30.9 reduce-scatter.42
  934.1 30.8 reduce-scatter.38
  967.9 57.0 reduce-scatter.28
  1028.4 57.0 reduce-scatter.20
  1088.4 57.0 reduce-scatter.26
  1148.9 57.0 reduce-scatter.24
  1209.5 57.0 reduce-scatter.22
  1269.7 120.7 reduce-scatter.30
  1393.5 120.7 reduce-scatter.32
  1517.3 120.7 reduce-scatter.34
  1641.4 24.5 reduce-scatter.40
  1669.0 310.1 all-reduce.8
